TPU v7x, 32 devices: a whole 2x2x4 slice. The times are simulated.
32 devices in a mesh: wide: 8 (over z, y), narrow: 4 (over x, core).
Axes of the slice: x: 2, y: 2, z: 4, core: 2. Of those that a mesh axis runs over, the one named last changes fastest.
Arguments:
- entry_factor: bfloat16 [288, 4, 64, 1024], P('wide', 'narrow'), may hold values from -6 to 6
- entry_panel: int32 [288, 4], P('wide', 'narrow'), may hold values from 0 to 1
- entry_target: int32 [288, 4], P('wide', 'narrow'), may hold values from 0 to 7, as said below
- entry_count: int32 [4, 8], P('narrow', 'wide'), may hold values from 1 to 36, 96 in all within a row
- panel_shared: bfloat16 [16, 64, 1024], P('wide', None, 'narrow'), may hold values from -0.1875 to 0.1875
- coupling: float32 [16, 64, 64], P('wide'), may hold values from -0.75 to 0.75
- probes: bfloat16 [32, 64, 1024], P('narrow'), may hold values from -6 to 6
Outputs:
- left_factor: float32 [32, 64, 1024], P('narrow', None, 'wide')
- right_factor: float32 [32, 64, 1024], P('narrow', None, 'wide')
Inputs may be any that keep to these rules, and one draw needn't show every extreme that they name: `entry_panel`: the local panel of an entry of any slot, live or not. `entry_target`: the local target of an entry; every target has at least one live entry. `entry_count`: the live slots of one device; for every owner the counts over the 8 wide indices sum to 96, and some device holds exactly 36.
All inputs are finite; a program needn't handle non-finite values.
Results may differ from a plain program's by a relative error of at most 0.0036.
Values may be sent and summed in bfloat16 or wider, within the bound.
A program may use at most 64 MiB of HBM per device.

v0:
```python
import math
import jax
import jax.numpy as jnp
from jax import lax
from jax.sharding import PartitionSpec as P


def shards(entry_factor, entry_panel, entry_target, entry_count, panel_shared, coupling, probes):
    highest = lax.Precision.HIGHEST
    factors = entry_factor[:, 0]
    slot_count = factors.shape[0]
    rank_dim = factors.shape[1]
    full_width = factors.shape[2]
    panel_count = panel_shared.shape[0]
    target_count = probes.shape[0]
    live_mask = (jnp.arange(slot_count) < entry_count[0, 0]).astype(jnp.float32)
    pick_panel = (entry_panel == jnp.arange(panel_count)[None, :]).astype(jnp.float32) * live_mask[
        :, None
    ]
    pick_target = (entry_target == jnp.arange(target_count)[None, :]).astype(jnp.float32)
    pair_pick = (pick_panel[:, :, None] * pick_target[:, None, :]).reshape(
        slot_count, panel_count * target_count
    )
    gathered = lax.all_gather(panel_shared, "narrow", axis=2, tiled=True)
    projected = jnp.einsum("drb,tkb->dtrk", gathered, probes, preferred_element_type=jnp.float32)
    coefficients = jnp.einsum("dij,dtjk->dtik", coupling, projected, precision=highest).astype(
        jnp.bfloat16
    )
    coeff_table = coefficients.reshape(panel_count * target_count, rank_dim * rank_dim)
    chosen = jnp.dot(
        pair_pick.astype(jnp.bfloat16), coeff_table, preferred_element_type=jnp.float32
    )
    chosen = chosen.astype(jnp.bfloat16).reshape(slot_count, rank_dim, rank_dim)
    contributions = jnp.einsum("eji,ejb->eib", chosen, factors, preferred_element_type=jnp.float32)
    sketch = jnp.einsum("et,eib->tib", pick_target, contributions, precision=highest)
    wide_count = lax.axis_size("wide")
    share_cols = full_width // wide_count
    sketch_sum = lax.psum(sketch, "wide")
    gram_matrix = jnp.einsum("tib,tjb->tij", sketch_sum, sketch_sum, precision=highest)
    lower_factor = jnp.linalg.cholesky(gram_matrix)
    basis = jax.scipy.linalg.solve_triangular(lower_factor, sketch_sum, lower=True)
    basis_round = basis.astype(jnp.bfloat16)
    own_basis = lax.dynamic_slice_in_dim(basis, lax.axis_index("wide") * share_cols, share_cols, 2)
    selected = jnp.einsum(
        "et,tkb->ekb",
        pick_target.astype(jnp.bfloat16),
        basis_round,
        preferred_element_type=jnp.float32,
    )
    selected = selected.astype(jnp.bfloat16)
    back_terms = jnp.einsum("eib,ekb->eik", factors, selected, preferred_element_type=jnp.float32)
    summed = jnp.einsum("ep,eik->pik", pair_pick, back_terms, precision=highest)
    summed = summed.reshape(panel_count, target_count, rank_dim, rank_dim)
    middle_terms = jnp.einsum("dtik,dij->dtkj", summed, coupling, precision=highest)
    partial_rows = jnp.einsum(
        "dtkj,djb->tkb", middle_terms, gathered.astype(jnp.float32), precision=highest
    )
    coeff_part = lax.psum_scatter(partial_rows, "wide", scatter_dimension=2, tiled=True)
    root_width = math.sqrt(full_width)
    return (own_basis * root_width, coeff_part / root_width)


def solution(mesh):
    placed = (
        P("wide", "narrow", None, None),
        P("wide", "narrow"),
        P("wide", "narrow"),
        P("narrow", "wide"),
        P("wide", None, "narrow"),
        P("wide", None, None),
        P("narrow", None, None),
    )
    return jax.shard_map(
        shards,
        mesh=mesh,
        in_specs=placed,
        out_specs=(P("narrow", None, "wide"), P("narrow", None, "wide")),
        check_vma=False,
    )
```

profile of v0, /device:TPU:0, one launch (start us, length us, event | category | flops | bytes accessed | tf_op | source)
XLA Modules:
  0.0 328.4 jit_solution(10725598671400621314)
XLA Ops:
  7.2 0.0 all-reduce.2.cloned.1.call-start
  7.2 0.7 fusion.36
  8.0 7.4 %all_gather.3 = bf16[2,64,1024]{2,1,0:T(8,128)(2,1)S(1)} all-gather(bf16[2,64,256]{2,1,0:T(8,128)(2,1)} %param.11), channel_id=1, replica_groups=mesh['wide'=8,'narrow'=4] {'narrow'}, dimensions={2}, use_global_device_ids=true | all-gather | bytes 327680 | tf_op jit(solution)/shard_map/all_gather | solution.py:24
  15.4 0.5 convolution_bitcast_fusion.1
  15.9 0.2 copy-done.2
  16.1 0.6 fusion.18
  16.7 0.2 copy.21
  16.9 0.3 reshape.98
  17.9 0.3 convolution_convert_fusion
  18.1 0.6 reshape.99
  18.8 3.8 %fusion.4 = f32[36,64,1024]{2,1,0:T(8,128)S(1)} fusion(bf16[36,64,64]{2,1,0:T(8,128)(2,1)S(1)} %reshape.99, bf16[36,1,64,1024]{3,2,1,0:T(8,128)(2,1)} %param.7), kind=kOutput, calls=%fused_computation.4 | convolution fusion | flops 301989888 | bytes 14450688 | tf_op jit(solution)/shard_map/eji,ejb->eib/dot_general | solution.py:34
  22.6 10.1 %fusion = f32[8,64,1024]{2,0,1:T(8,128)} fusion(f32[36,64,1024]{2,1,0:T(8,128)S(1)} %fusion.4, s32[36]{0:T(128)S(1)} %bitcast.78), kind=kOutput, calls=%fused_computation | convolution fusion | flops 226492704 | bytes 11534480 | tf_op jit(solution)/shard_map/et,eib->tib/dot_general | solution.py:35
  32.7 0.0 reduce-scatter.2.cloned.1.call-start
  32.8 103.7 %all-reduce.2.cloned.1.call-done = f32[8,64,1024]{2,0,1:T(8,128)} async-done(((f32[8,64,1024]{2,0,1:T(8,128)}), f32[8,64,1024]{2,0,1:T(8,128)}) %all-reduce.2.cloned.1.call-update) | async-done | bytes 2097168 | tf_op jit(solution)/shard_map/psum | solution.py:38
  136.4 6.7 %fusion.9 = f32[8,64,64]{2,1,0:T(8,128)S(1)} fusion(f32[8,64,1024]{2,0,1:T(8,128)} %all-reduce.2.cloned.1.call-done), kind=kOutput, calls=%fused_computation.11 | convolution fusion | flops 402653184 | bytes 2228224 | tf_op jit(solution)/shard_map/tib,tjb->tij/dot_general | solution.py:39
  143.1 0.8 copy.26
  144.0 1.7 fusion.25
  145.7 47.6 %custom-call.8 = f32[8,64,64]{2,1,0:T(8,128)S(1)} custom-call(f32[8,64,64]{2,1,0:T(8,128)} %fusion.25), custom_call_target="Cholesky" | custom-call | tf_op jit(solution)/shard_map/jit(cholesky)/cholesky | solution.py:40
  193.3 0.1 compare_reduce_fusion
  193.4 0.8 select_bitcast_fusion
  194.3 40.3 %custom-call.9 = f32[8,1,64,64]{2,3,1,0:T(8,128)S(1)} custom-call(f32[8,1,64,64]{3,2,1,0:T(8,128)} %select_bitcast_fusion), custom_call_target="InvertDiagBlocksLowerTriangular" | custom-call | tf_op jit(solution)/shard_map/jit(_solve_triangular)/vmap()/triangular_solve | solution.py:41
  234.5 4.4 %fusion.42 = (bf16[8,64,1024]{2,1,0:T(8,128)(2,1)S(1)}, f32[8,64,1024]{2,1,0:T(8,128)}) fusion(f32[8,64,1024]{2,0,1:T(8,128)S(1)} %copy-done.1, f32[8,1,64,64]{2,3,1,0:T(8,128)S(1)} %custom-call.9), kind=kOutput, calls=%fused_computation.53 | convolution fusion | flops 403177472 | bytes 5373952 | tf_op jit(solution)/shard_map/jit(_solve_triangular)/vmap()/triangular_solve | solution.py:41
  238.9 1.6 convolution_convert_fusion.1
  240.5 5.5 %fusion.11 = f32[36,64,64]{1,2,0:T(8,128)S(1)} fusion(bf16[36,1,64,1024]{3,2,1,0:T(8,128)(2,1)} %param.7, bf16[36,64,1024]{2,0,1:T(8,128)(2,1)S(1)} %convolution_convert_fusion.1), kind=kOutput, calls=%fused_computation.14 | convolution fusion | flops 301989888 | bytes 10027008 | tf_op jit(solution)/shard_map/eib,ekb->eik/dot_general | solution.py:51
  246.0 0.5 copy.31
  246.5 0.8 fusion.16
  247.3 1.8 fusion.21
  249.1 2.3 convolution_bitcast_fusion
  251.4 0.0 reduce-scatter.2.cloned.1.call-update
  251.5 1.7 dynamic-slice_multiply_fusion
  253.1 66.7 %reduce-scatter.2.cloned.1.call-done = f32[8,64,128]{2,1,0:T(8,128)} async-done(((f32[8,64,1024]{2,1,0:T(8,128)}), f32[8,64,128]{2,1,0:T(8,128)}) %reduce-scatter.2.cloned.1.call-update) | async-done | bytes 262160 | tf_op jit(solution)/shard_map/reduce_scatter | solution.py:58
  319.8 1.7 broadcast_multiply_fusion
  (19 shorter events, 0.1 us)
Async XLA Ops:
  7.2 8.2 %copy-start = (bf16[8,64,1024]{2,1,0:T(8,128)(2,1)S(1)}, bf16[8,64,1024]{2,1,0:T(8,128)(2,1)}, u32[]{:S(2)}) copy-start(bf16[8,64,1024]{2,1,0:T(8,128)(2,1)} %param.13) | copy-start | bytes 3145732
  7.2 8.9 %copy-start.4 = (f32[2,64,64]{2,1,0:T(8,128)S(1)}, f32[2,64,64]{2,1,0:T(8,128)}, u32[]{:S(2)}) copy-start(f32[2,64,64]{2,1,0:T(8,128)} %param.12) | copy-start | bytes 98308
  7.2 10.6 %copy-start.6 = (s32[36,1]{0,1:T(1,128)S(1)}, s32[36,1]{0,1:T(1,128)}, u32[]{:S(2)}) copy-start(s32[36,1]{0,1:T(1,128)} %param.8) | copy-start | bytes 436
  7.2 129.2 %all-reduce.2.cloned.1.call-start = ((), (), s32[]{:S(2)}) async-start(), calls=%async_computation.1 | async-start | bytes 4194304 | tf_op jit(solution)/shard_map/psum | solution.py:38
  15.4 0.7 copy-start.2
  18.8 3.8 %copy-start.5 = (s32[36,1]{0,1:T(1,128)S(1)}, s32[36,1]{0,1:T(1,128)}, u32[]{:S(2)}) copy-start(s32[36,1]{0,1:T(1,128)} %param.9) | copy-start | bytes 436
  32.7 287.2 %reduce-scatter.2.cloned.1.call-start = ((), (), s32[]{:S(2)}) async-start(), calls=%async_computation.2 | async-start | bytes 2359296 | tf_op jit(solution)/shard_map/reduce_scatter | solution.py:58
  136.4 98.1 %copy-start.1 = (f32[8,64,1024]{2,0,1:T(8,128)S(1)}, f32[8,64,1024]{2,0,1:T(8,128)}, u32[]{:S(2)}) copy-start(f32[8,64,1024]{2,0,1:T(8,128)} %all-reduce.2.cloned.1.call-done) | copy-start | bytes 6291460
  246.5 2.6 copy-start.3
Sparse Core Ops, SparseCore 0:
  32.8 103.5 all-reduce.1
  251.6 68.2 reduce-scatter.1
where the time goes:
time: 329 us; the launch traced here: 328 us
  waiting for transfers between devices  170 us (52%)
  other arithmetic  94.6 us (29%)
  matrix products  38.3 us (12%)
  between operations  14.9 us (5%)
  blocking collectives  7.42 us (2%)
    psum x1, waiting for transfers between devices, shards(): sketch_sum = lax.psum(sketch, 'wide')  104 us
    reduce_scatter x1, waiting for transfers between devices, shards(): lax.psum_scatter(partial_rows, 'wide', scatter_dimension=2, tiled=True)  66.7 us
    another operation x4, other arithmetic, shards(): lower_factor = jnp.linalg.cholesky(gram_matrix)  47.8 us
    another operation x3, other arithmetic, shards(): jax.scipy.linalg.solve_triangular(lower_factor, sketch_sum, lower=True)  41.1 us
    dot_general x1, matrix products, shards(): jnp.einsum('et,eib->tib', pick_target, contributions, precision=highest)  10.1 us
    all_gather x1, blocking collectives, shards(): gathered = lax.all_gather(panel_shared, 'narrow', axis=2, tiled=True)  7.42 us
    dot_general x1, matrix products, shards(): jnp.einsum('tib,tjb->tij', sketch_sum, sketch_sum, precision=highest)  6.7 us
  transfers between devices with their start and end apart: 2, of which 2 were waited for; matrix products, arithmetic and copies ran while one was open for 1% of the time, Pallas kernels for 0%

commit v1 on v0

--- a/solution.py
+++ b/solution.py
@@ -35,7 +35,7 @@
     sketch = jnp.einsum("et,eib->tib", pick_target, contributions, precision=highest)
     wide_count = lax.axis_size("wide")
     share_cols = full_width // wide_count
-    sketch_sum = lax.psum(sketch, "wide")
+    sketch_sum = jnp.sum(lax.all_gather(sketch, "wide"), axis=0)
     gram_matrix = jnp.einsum("tib,tjb->tij", sketch_sum, sketch_sum, precision=highest)
     lower_factor = jnp.linalg.cholesky(gram_matrix)
     basis = jax.scipy.linalg.solve_triangular(lower_factor, sketch_sum, lower=True)

time: 329 us -> 459 us (1.40)
  waiting for transfers between devices: 170 us -> 294 us
  other arithmetic: 94.6 us -> 103 us
    all_gather x0 -> x1, waiting for transfers between devices: none -> 229 us  [shards(): sketch_sum = jnp.sum(lax.all_gather(sketch, 'wide'), axis=0)]
    psum x1 -> x0, waiting for transfers between devices: 104 us -> none  [shards(): sketch_sum = lax.psum(sketch, 'wide')]
    reduce_sum x0 -> x1, other arithmetic: none -> 8.23 us  [shards(): sketch_sum = jnp.sum(lax.all_gather(sketch, 'wide'), axis=0)]
  transfers between devices with their start and end apart: 2 -> 2, of which waited for: 2 -> 2; matrix products, arithmetic and copies ran while one was open for 1% -> 0% of each run, Pallas kernels for 0% -> 0%
where the time goes in v1:
time: 459 us; the launch traced here: 458 us
  waiting for transfers between devices  294 us (64%)
  other arithmetic  103 us (22%)
  matrix products  36 us (8%)
  between operations  14.9 us (3%)
  blocking collectives  7.42 us (2%)
    all_gather x1, waiting for transfers between devices, shards(): sketch_sum = jnp.sum(lax.all_gather(sketch, 'wide'), axis=0)  229 us
    reduce_scatter x1, waiting for transfers between devices, shards(): lax.psum_scatter(partial_rows, 'wide', scatter_dimension=2, tiled=True)  65.7 us
    another operation x4, other arithmetic, shards(): lower_factor = jnp.linalg.cholesky(gram_matrix)  47.8 us
    another operation x3, other arithmetic, shards(): jax.scipy.linalg.solve_triangular(lower_factor, sketch_sum, lower=True)  41.1 us
    dot_general x1, matrix products, shards(): jnp.einsum('et,eib->tib', pick_target, contributions, precision=highest)  10.1 us
  transfers between devices with their start and end apart: 2, of which 2 were waited for; matrix products, arithmetic and copies ran while one was open for 0% of the time, Pallas kernels for 0%

profile of v1, /device:TPU:0, one launch (start us, length us, event | category | flops | bytes accessed | tf_op | source)
XLA Modules:
  0.0 458.2 jit_solution(83625696495549002)
XLA Ops:
  7.2 0.0 all-gather.3.cloned.1.call-start
  7.2 0.7 fusion.36
  8.0 7.4 %all_gather.9 = bf16[2,64,1024]{2,1,0:T(8,128)(2,1)S(1)} all-gather(bf16[2,64,256]{2,1,0:T(8,128)(2,1)} %param.11), channel_id=1, replica_groups=mesh['wide'=8,'narrow'=4] {'narrow'}, dimensions={2}, use_global_device_ids=true | all-gather | bytes 327680 | tf_op jit(solution)/shard_map/all_gather | solution.py:24
  15.4 0.5 convolution_bitcast_fusion.1
  15.9 0.2 copy-done.1
  16.1 0.6 fusion.18
  16.7 0.2 copy.27
  16.9 0.3 reshape.98
  17.9 0.3 convolution_convert_fusion
  18.1 0.6 reshape.99
  18.8 3.8 fusion.4
  22.6 10.1 %fusion = f32[8,64,1024]{2,0,1:T(8,128)} fusion(f32[36,64,1024]{2,1,0:T(8,128)S(1)} %fusion.4, s32[36]{0:T(128)S(1)} %bitcast.80), kind=kOutput, calls=%fused_computation.1 | convolution fusion | flops 226492704 | bytes 11534480 | tf_op jit(solution)/shard_map/et,eib->tib/dot_general | solution.py:35
  32.7 0.0 reduce-scatter.2.cloned.1.call-start
  32.8 228.6 %all-gather.3.cloned.1.call-done = f32[64,64,1024]{2,0,1:T(8,128)} async-done(((f32[8,64,1024]{2,0,1:T(8,128)}), f32[64,64,1024]{2,0,1:T(8,128)}) %all-gather.3.cloned.1.call-update) | async-done | bytes 16777232 | tf_op jit(solution)/shard_map/all_gather | solution.py:38
  261.4 8.2 %bitcast_reduce_fusion = f32[8,64,1024]{2,0,1:T(8,128)S(1)} fusion(f32[64,64,1024]{2,0,1:T(8,128)} %all-gather.3.cloned.1.call-done), kind=kLoop, calls=%fused_computation | loop fusion | flops 3670016 | bytes 18874368 | tf_op jit(solution)/shard_map/reduce_sum | solution.py:38
  269.7 4.4 fusion.9
  274.0 0.8 copy.32
  274.9 1.7 fusion.25
  276.6 47.6 %custom-call.8 = f32[8,64,64]{2,1,0:T(8,128)S(1)} custom-call(f32[8,64,64]{2,1,0:T(8,128)} %fusion.25), custom_call_target="Cholesky" | custom-call | tf_op jit(solution)/shard_map/jit(cholesky)/cholesky | solution.py:40
  324.2 0.1 compare_reduce_fusion
  324.3 0.8 select_bitcast_fusion
  325.2 40.3 %custom-call.9 = f32[8,1,64,64]{2,3,1,0:T(8,128)S(1)} custom-call(f32[8,1,64,64]{3,2,1,0:T(8,128)} %select_bitcast_fusion), custom_call_target="InvertDiagBlocksLowerTriangular" | custom-call | tf_op jit(solution)/shard_map/jit(_solve_triangular)/vmap()/triangular_solve | solution.py:41
  365.4 4.4 fusion.42
  369.8 1.6 convolution_convert_fusion.1
  371.4 5.5 %fusion.11 = f32[36,64,64]{1,2,0:T(8,128)S(1)} fusion(bf16[36,1,64,1024]{3,2,1,0:T(8,128)(2,1)} %param.7, bf16[36,64,1024]{2,0,1:T(8,128)(2,1)S(1)} %convolution_convert_fusion.1), kind=kOutput, calls=%fused_computation.15 | convolution fusion | flops 301989888 | bytes 10027008 | tf_op jit(solution)/shard_map/eib,ekb->eik/dot_general | solution.py:51
  376.9 0.5 copy.37
  377.4 0.8 fusion.16
  378.1 1.8 fusion.21
  380.0 2.3 convolution_bitcast_fusion
  382.4 1.7 dynamic-slice_multiply_fusion
  384.0 65.7 %reduce-scatter.2.cloned.1.call-done = f32[8,64,128]{2,1,0:T(8,128)} async-done(((f32[8,64,1024]{2,1,0:T(8,128)}), f32[8,64,128]{2,1,0:T(8,128)}) %reduce-scatter.2.cloned.1.call-update) | async-done | bytes 262160 | tf_op jit(solution)/shard_map/reduce_scatter | solution.py:58
  449.7 1.7 broadcast_multiply_fusion
  (18 shorter events, 0.1 us)
Async XLA Ops:
  7.2 8.2 %copy-start = (bf16[8,64,1024]{2,1,0:T(8,128)(2,1)S(1)}, bf16[8,64,1024]{2,1,0:T(8,128)(2,1)}, u32[]{:S(2)}) copy-start(bf16[8,64,1024]{2,1,0:T(8,128)(2,1)} %param.13) | copy-start | bytes 3145732
  7.2 8.9 %copy-start.3 = (f32[2,64,64]{2,1,0:T(8,128)S(1)}, f32[2,64,64]{2,1,0:T(8,128)}, u32[]{:S(2)}) copy-start(f32[2,64,64]{2,1,0:T(8,128)} %param.12) | copy-start | bytes 98308
  7.2 10.6 %copy-start.5 = (s32[36,1]{0,1:T(1,128)S(1)}, s32[36,1]{0,1:T(1,128)}, u32[]{:S(2)}) copy-start(s32[36,1]{0,1:T(1,128)} %param.8) | copy-start | bytes 436
  7.2 254.2 %all-gather.3.cloned.1.call-start = ((), (), s32[]{:S(2)}) async-start(), calls=%async_computation.2 | async-start | bytes 18874368 | tf_op jit(solution)/shard_map/all_gather | solution.py:38
  15.4 0.7 copy-start.1
  18.8 3.8 copy-start.4
  32.7 417.0 %reduce-scatter.2.cloned.1.call-start = ((), (), s32[]{:S(2)}) async-start(), calls=%async_computation.1 | async-start | bytes 2359296 | tf_op jit(solution)/shard_map/reduce_scatter | solution.py:58
  377.4 2.6 copy-start.2
Sparse Core Ops, SparseCore 0:
  32.8 228.5 all-gather.2
  382.5 67.1 reduce-scatter.1
